TPU v7x, 256 devices: a whole 4x4x8 slice. The times are simulated.
256 devices in a mesh: dp: 16 (over y, x), expert: 16 (over z, core).
Axes of the slice: x: 4, y: 4, z: 8, core: 2. Of those that a mesh axis runs over, the one named last changes fastest.
Arguments:
- tokens: bfloat16 [16384, 2048], P(('dp', 'expert')), may hold values from -6 to 6
- expert_ids: int32 [16384, 8], P(('dp', 'expert')), may hold values from 0 to 127, all different within a row; in each aligned block of 32 rows (0 to 31, 32 to 63, ...) at most 3 rows name the same one
- gate_fixed: int32 [16384, 8], P(('dp', 'expert')), may hold values from 1 to 65535
- w_gate: bfloat16 [256, 2048, 384], P(('dp', 'expert')), may hold values from -0.125 to 0.125
- w_up: bfloat16 [256, 2048, 384], P(('dp', 'expert')), may hold values from -0.125 to 0.125
- w_down: bfloat16 [256, 384, 2048], P(('dp', 'expert')), may hold values from -0.21875 to 0.21875
Outputs:
- mixed: float32 [16384, 2048], P(('dp', 'expert'))
Inputs may be any that keep to these rules, and one draw needn't show every extreme that they name: `expert_ids`: each row names 8 different experts. In each aligned block of 32 rows (the first or the second half of one device's rows) no expert is named by more than 3 rows, a bound that some block reaches.
All inputs are finite; a program needn't handle non-finite values.
Results may differ from a plain program's by a relative error of at most 0.0041.
Values may be sent and summed in bfloat16 or wider, within the bound.
No kernel may reach another device: no remote copies, remote signals or barrier semaphores. Data moves between devices by JAX's collectives and lax.ppermute only.
A program may use at most 64 MiB of HBM per device.

v0:
```python
import jax
import jax.numpy as jnp
from jax import lax
from jax.sharding import PartitionSpec as P


def partner(x, axis, stride):
    return lax.ppermute(x, axis, [(i, i ^ 1 << stride) for i in range(lax.axis_size(axis))])


def per_device(tokens, expert_ids, gate_fixed, w_gate, w_up, w_down):
    dp_count = lax.axis_size("dp")
    col_count = lax.axis_size("expert")
    pair_count = col_count // 2
    dev_count = dp_count * col_count
    expert_count = dev_count // 2
    token_count, width = tokens.shape
    choice_count = expert_ids.shape[1]
    capacity = 3 * token_count * choice_count // (4 * expert_count)
    half_rows = token_count // 2
    other_gate, other_up, other_down = partner((w_gate[0], w_up[0], w_down[0]), "expert", 0)
    gate_full = jnp.concatenate([w_gate[0], other_gate], axis=1)
    up_full = jnp.concatenate([w_up[0], other_up], axis=1)
    down_full = jnp.concatenate([w_down[0], other_down], axis=0)
    gates = gate_fixed.astype(jnp.float32)
    mix_weight = gates / jnp.sum(gates, axis=1, keepdims=True)
    flat_ids = expert_ids.reshape(-1)
    choice_pos = jnp.arange(token_count * choice_count, dtype=jnp.int32)
    half_index = choice_pos // choice_count // half_rows
    onehot = (flat_ids[:, None] == jnp.arange(expert_count, dtype=jnp.int32)[None, :]).astype(
        jnp.int32
    )
    onehot = onehot.reshape(2, half_rows * choice_count, expert_count)
    earlier = jnp.cumsum(onehot, axis=1) - onehot
    slot_index = jnp.sum(earlier * onehot, axis=2).reshape(-1)
    dest_dp = flat_ids // pair_count
    dest_col = 2 * (flat_ids % pair_count) + half_index
    target = (dest_dp * col_count + dest_col) * capacity + slot_index
    repeated = jnp.repeat(tokens, choice_count, axis=0)
    outgoing = jnp.zeros((dev_count * capacity, width), jnp.bfloat16).at[target].set(repeated)
    outgoing = outgoing.reshape(dp_count, col_count, capacity, width)
    first_section = lax.all_to_all(outgoing, "dp", split_axis=0, concat_axis=0, tiled=True)
    arrived = lax.all_to_all(first_section, "expert", split_axis=1, concat_axis=1, tiled=True)
    shape_in = arrived.shape
    token_rows = arrived.reshape(-1, width)
    gate_part = jnp.dot(token_rows, gate_full, preferred_element_type=jnp.float32)
    up_part = jnp.dot(token_rows, up_full, preferred_element_type=jnp.float32)
    hidden = (jax.nn.silu(gate_part) * up_part).astype(jnp.bfloat16)
    expert_out = jnp.dot(hidden, down_full, preferred_element_type=jnp.float32).astype(jnp.bfloat16)
    returned = lax.all_to_all(
        expert_out.reshape(shape_in), "expert", split_axis=1, concat_axis=1, tiled=True
    )
    home = lax.all_to_all(returned, "dp", split_axis=0, concat_axis=0, tiled=True)
    home_flat = home.reshape(dev_count * capacity, width)
    picked = home_flat[target].reshape(token_count, choice_count, width)
    mixed = jnp.sum(picked.astype(jnp.float32) * mix_weight[:, :, None], axis=1)
    return mixed


def solution(mesh):
    placed = (
        P(("dp", "expert"), None),
        P(("dp", "expert"), None),
        P(("dp", "expert"), None),
        P(("dp", "expert"), None, None),
        P(("dp", "expert"), None, None),
        P(("dp", "expert"), None, None),
    )
    return jax.shard_map(
        per_device, mesh=mesh, in_specs=placed, out_specs=P(("dp", "expert"), None), check_vma=False
    )
```

profile of v0, /device:TPU:1, one launch (start us, length us, event | category | flops | bytes accessed | tf_op | source)
XLA Modules:
  0.0 335.0 jit_solution(7348025419594827379)
XLA Ops:
  0.0 0.8 copy.14
  1.2 0.4 fusion.17
  2.2 4.6 %scatter_custom_fusion = bf16[768,2048]{1,0:T(8,128)(2,1)S(1)} fusion(s32[512]{0:T(512)S(1)} %bitcast.27, bf16[]{:T(256)} %constant.54.clone.1, bf16[64,2048]{1,0:T(8,128)(2,1)S(1)} %copy-done), kind=kCustom, calls=%fused_computation.17 | custom fusion | bytes 3407874 | tf_op jit(solution)/shard_map/scatter | solution.py:40
  6.8 4.4 %reshape.259 = bf16[16,16,3,2048]{3,2,1,0:T(4,128)(2,1)} reshape(bf16[768,2048]{1,0:T(8,128)(2,1)S(1)} %scatter_custom_fusion) | data formatting | bytes 6291456 | tf_op jit(solution)/shard_map/reshape | solution.py:41
  11.2 4.7 %copy.19 = bf16[16,16,3,2048]{3,1,2,0:T(8,128)(2,1)S(1)} copy(bf16[16,16,3,2048]{3,2,1,0:T(4,128)(2,1)} %reshape.259) | data formatting | bytes 6291456 | tf_op jit(solution)/shard_map/reshape | solution.py:41
  15.9 46.0 %all_to_all.20 = bf16[16,16,3,2048]{3,1,2,0:T(8,128)(2,1)S(1)} all-to-all(bf16[16,16,3,2048]{3,1,2,0:T(8,128)(2,1)S(1)} %copy.19), channel_id=1, replica_groups=mesh['dp'=16,'expert'=16] {'dp'}, dimensions={0} | all-to-all | bytes 6291456 | tf_op jit(solution)/shard_map/all_to_all | solution.py:42
  61.9 3.4 %copy.20 = bf16[16,16,3,2048]{3,0,2,1:T(8,128)(2,1)} copy(bf16[16,16,3,2048]{3,1,2,0:T(8,128)(2,1)S(1)} %all_to_all.20) | data formatting | bytes 6291456 | tf_op jit(solution)/shard_map/all_to_all | solution.py:42
  65.3 10.5 %all-to-all-start.1 = ((bf16[16,16,3,2048]{3,0,2,1:T(8,128)(2,1)}), bf16[16,16,3,2048]{3,0,2,1:T(8,128)(2,1)S(1)}, u32[]{:S(2)}, u32[]{:S(2)}) async-start(bf16[16,16,3,2048]{3,0,2,1:T(8,128)(2,1)} %copy.20), calls=%async_computation.1 | async-start | bytes 6291456 | tf_op jit(solution)/shard_map/all_to_all | solution.py:43
  76.5 70.3 %all-to-all-done.1 = bf16[16,16,3,2048]{3,0,2,1:T(8,128)(2,1)S(1)} async-done(((bf16[16,16,3,2048]{3,0,2,1:T(8,128)(2,1)}), bf16[16,16,3,2048]{3,0,2,1:T(8,128)(2,1)S(1)}, u32[]{:S(2)}, u32[]{:S(2)}) %all-to-all-start.1) | async-done | bytes 3145760 | tf_op jit(solution)/shard_map/all_to_all | solution.py:43
  146.8 4.6 %copy.21 = bf16[16,16,3,2048]{3,2,1,0:T(4,128)(2,1)} copy(bf16[16,16,3,2048]{3,0,2,1:T(8,128)(2,1)S(1)} %all-to-all-done.1) | data formatting | bytes 6291456 | tf_op jit(solution)/shard_map/all_to_all | solution.py:43
  151.4 7.5 %reshape.260 = bf16[768,2048]{1,0:T(8,128)(2,1)S(1)} reshape(bf16[16,16,3,2048]{3,2,1,0:T(4,128)(2,1)} %copy.21) | data formatting | bytes 6291456 | tf_op jit(solution)/shard_map/reshape | solution.py:45
  158.9 4.6 %fusion.1 = f32[768,768]{1,0:T(8,128)S(1)} fusion(bf16[768,2048]{1,0:T(8,128)(2,1)S(1)} %reshape.260, bf16[2048,384]{1,0:T(8,128)(2,1)} %collective-permute-done, bf16[2048,384]{1,0:T(8,128)(2,1)} %bitcast.31), kind=kOutput, calls=%fused_computation.5 | convolution fusion | flops 2422210560 | bytes 8650752 | tf_op jit(solution)/shard_map/dot_general | solution.py:46
  163.5 4.1 %fusion.5 = f32[768,768]{1,0:T(8,128)S(1)} fusion(bf16[768,2048]{1,0:T(8,128)(2,1)S(1)} %reshape.260, bf16[2048,384]{1,0:T(8,128)(2,1)} %collective-permute-done.1, bf16[2048,384]{1,0:T(8,128)(2,1)S(1)} %bitcast.33), kind=kOutput, calls=%fused_computation.9 | convolution fusion | flops 2422210560 | bytes 8650752 | tf_op jit(solution)/shard_map/dot_general | solution.py:47
  167.7 4.1 %convolution_convert_fusion = bf16[768,2048]{1,0:T(8,128)(2,1)S(1)} fusion(bf16[384,2048]{1,0:T(8,128)(2,1)} %collective-permute-done.2, bf16[384,2048]{1,0:T(8,128)(2,1)S(1)} %bitcast.35, f32[768,768]{1,0:T(8,128)S(1)} %fusion.5, f32[768,768]{1,0:T(8,128)S(1)} %fusion.1), kind=kOutput, calls=%fused_computation.4 | convolution fusion | flops 2427322368 | bytes 11010048 | tf_op jit(solution)/shard_map/dot_general | solution.py:49
  171.8 4.4 %reshape.261 = bf16[16,16,3,2048]{3,2,1,0:T(4,128)(2,1)} reshape(bf16[768,2048]{1,0:T(8,128)(2,1)S(1)} %convolution_convert_fusion) | data formatting | bytes 6291456 | tf_op jit(solution)/shard_map/reshape | solution.py:51
  176.2 4.7 %copy.22 = bf16[16,16,3,2048]{3,0,2,1:T(8,128)(2,1)S(1)} copy(bf16[16,16,3,2048]{3,2,1,0:T(4,128)(2,1)} %reshape.261) | data formatting | bytes 6291456 | tf_op jit(solution)/shard_map/reshape | solution.py:51
  180.9 78.7 %all_to_all.21 = bf16[16,16,3,2048]{3,0,2,1:T(8,128)(2,1)S(1)} all-to-all(bf16[16,16,3,2048]{3,0,2,1:T(8,128)(2,1)S(1)} %copy.22), channel_id=1, replica_groups=mesh['dp'=16,'expert'=16] {'expert'}, dimensions={1} | all-to-all | bytes 6291456 | tf_op jit(solution)/shard_map/all_to_all | solution.py:50
  259.6 3.4 %copy.23 = bf16[16,16,3,2048]{3,1,2,0:T(8,128)(2,1)} copy(bf16[16,16,3,2048]{3,0,2,1:T(8,128)(2,1)S(1)} %all_to_all.21) | data formatting | bytes 6291456 | tf_op jit(solution)/shard_map/all_to_all | solution.py:50
  263.0 4.1 %all-to-all-start.3 = ((bf16[16,16,3,2048]{3,1,2,0:T(8,128)(2,1)}), bf16[16,16,3,2048]{3,1,2,0:T(8,128)(2,1)S(1)}, u32[]{:S(2)}, u32[]{:S(2)}) async-start(bf16[16,16,3,2048]{3,1,2,0:T(8,128)(2,1)} %copy.23), calls=%async_computation.3 | async-start | bytes 6291456 | tf_op jit(solution)/shard_map/all_to_all | solution.py:53
  267.3 47.9 %all-to-all-done.3 = bf16[16,16,3,2048]{3,1,2,0:T(8,128)(2,1)S(1)} async-done(((bf16[16,16,3,2048]{3,1,2,0:T(8,128)(2,1)}), bf16[16,16,3,2048]{3,1,2,0:T(8,128)(2,1)S(1)}, u32[]{:S(2)}, u32[]{:S(2)}) %all-to-all-start.3) | async-done | bytes 3145760 | tf_op jit(solution)/shard_map/all_to_all | solution.py:53
  315.2 4.7 %copy.24 = bf16[16,16,3,2048]{3,2,1,0:T(4,128)(2,1)} copy(bf16[16,16,3,2048]{3,1,2,0:T(8,128)(2,1)S(1)} %all-to-all-done.3) | data formatting | bytes 6291456 | tf_op jit(solution)/shard_map/all_to_all | solution.py:53
  319.9 7.5 %reshape.262 = bf16[768,2048]{1,0:T(8,128)(2,1)S(1)} reshape(bf16[16,16,3,2048]{3,2,1,0:T(4,128)(2,1)} %copy.24) | data formatting | bytes 6291456 | tf_op jit(solution)/shard_map/reshape | solution.py:54
  327.4 3.3 gather_fusion
  330.7 4.2 %fusion = f32[64,2048]{1,0:T(8,128)} fusion(bf16[512,2048]{1,0:T(8,128)(2,1)} %gather_fusion, f32[64,8]{1,0:T(8,128)S(1)} %copy.25), kind=kLoop, calls=%fused_computation.3 | loop fusion | flops 3014656 | bytes 2623488 | tf_op jit(solution)/shard_map/reduce_sum | solution.py:56
  (32 shorter events, 1.7 us)
Async XLA Ops:
  0.0 2.2 copy-start
  65.3 81.4 %all-to-all-start.1 = ((bf16[16,16,3,2048]{3,0,2,1:T(8,128)(2,1)}), bf16[16,16,3,2048]{3,0,2,1:T(8,128)(2,1)S(1)}, u32[]{:S(2)}, u32[]{:S(2)}) async-start(bf16[16,16,3,2048]{3,0,2,1:T(8,128)(2,1)} %copy.20), calls=%async_computation.1 | async-start | bytes 6291456 | tf_op jit(solution)/shard_map/all_to_all | solution.py:43
  75.8 83.1 %collective-permute-start = (bf16[2048,384]{1,0:T(8,128)(2,1)}, bf16[2048,384]{1,0:T(8,128)(2,1)}, u32[]{:S(2)}, u32[]{:S(2)}) collective-permute-start(bf16[2048,384]{1,0:T(8,128)(2,1)} %bitcast.30), channel_id=1, source_target_pairs={{0,1},{1,0},{2,3},{3,2},{4,5},{5,4},{6,7},{7,6},{8,9},{9,8},{10,11... | collective-permute-start | bytes 4718600 | tf_op jit(solution)/shard_map/ppermute | solution.py:8
  76.0 87.6 %collective-permute-start.1 = (bf16[2048,384]{1,0:T(8,128)(2,1)}, bf16[2048,384]{1,0:T(8,128)(2,1)}, u32[]{:S(2)}, u32[]{:S(2)}) collective-permute-start(bf16[2048,384]{1,0:T(8,128)(2,1)} %bitcast.32), channel_id=1, source_target_pairs={{0,1},{1,0},{2,3},{3,2},{4,5},{5,4},{6,7},{7,6},{8,9},{9,8},{10,11... | collective-permute-start | bytes 4718600 | tf_op jit(solution)/shard_map/ppermute | solution.py:8
  76.3 91.4 %collective-permute-start.2 = (bf16[384,2048]{1,0:T(8,128)(2,1)}, bf16[384,2048]{1,0:T(8,128)(2,1)}, u32[]{:S(2)}, u32[]{:S(2)}) collective-permute-start(bf16[384,2048]{1,0:T(8,128)(2,1)} %bitcast.34), channel_id=1, source_target_pairs={{0,1},{1,0},{2,3},{3,2},{4,5},{5,4},{6,7},{7,6},{8,9},{9,8},{10,11... | collective-permute-start | bytes 4718600 | tf_op jit(solution)/shard_map/ppermute | solution.py:8
  158.9 4.6 %copy-start.3 = (bf16[1,2048,384]{2,1,0:T(8,128)(2,1)S(1)}, bf16[1,2048,384]{2,1,0:T(8,128)(2,1)}, u32[]{:S(2)}) copy-start(bf16[1,2048,384]{2,1,0:T(8,128)(2,1)} %param.10) | copy-start | bytes 4718596
  163.5 4.2 %copy-start.4 = (bf16[1,384,2048]{2,1,0:T(8,128)(2,1)S(1)}, bf16[1,384,2048]{2,1,0:T(8,128)(2,1)}, u32[]{:S(2)}) copy-start(bf16[1,384,2048]{2,1,0:T(8,128)(2,1)} %param.11) | copy-start | bytes 4718596
  263.0 4.1 %copy-start.2 = (s32[64,8]{0,1:T(8,128)S(1)}, s32[64,8]{0,1:T(8,128)}, u32[]{:S(2)}) copy-start(s32[64,8]{0,1:T(8,128)} %param.8) | copy-start | bytes 6148
  263.0 52.1 %all-to-all-start.3 = ((bf16[16,16,3,2048]{3,1,2,0:T(8,128)(2,1)}), bf16[16,16,3,2048]{3,1,2,0:T(8,128)(2,1)S(1)}, u32[]{:S(2)}, u32[]{:S(2)}) async-start(bf16[16,16,3,2048]{3,1,2,0:T(8,128)(2,1)} %copy.23), calls=%async_computation.3 | async-start | bytes 6291456 | tf_op jit(solution)/shard_map/all_to_all | solution.py:53
  327.4 7.6 %copy-start.1 = (bf16[64,2048]{1,0:T(8,128)(2,1)S(1)}, bf16[64,2048]{1,0:T(8,128)(2,1)}, u32[]{:S(2)}) copy-start(bf16[64,2048]{1,0:T(8,128)(2,1)} %param.6) | copy-start | bytes 786436
where the time goes:
time: 336 us; the launch traced here: 335 us
  blocking collectives  125 us (37%)
  waiting for transfers between devices  118 us (35%)
  local copies, waits for them, and re-layouts  58.7 us (17%)
  starting transfers between devices  15.3 us (5%)
  matrix products  12.8 us (4%)
  other arithmetic  5.1 us (2%)
    all_to_all x1, blocking collectives, per_device(): lax.all_to_all(expert_out.reshape(shape_in), 'expert', split_axis=1, conc...  78.7 us
    all_to_all x1, waiting for transfers between devices, per_device(): lax.all_to_all(first_section, 'expert', split_axis=1, concat_axis=1, tile...  70.3 us
    all_to_all x1, waiting for transfers between devices, per_device(): lax.all_to_all(returned, 'dp', split_axis=0, concat_axis=0, tiled=True)  47.9 us
    all_to_all x1, blocking collectives, per_device(): lax.all_to_all(outgoing, 'dp', split_axis=0, concat_axis=0, tiled=True)  46 us
    all_to_all x1, starting transfers between devices, per_device(): lax.all_to_all(first_section, 'expert', split_axis=1, concat_axis=1, tile...  10.5 us
    reshape x2, local copies, waits for them, and re-layouts, per_device(): expert_out.reshape(shape_in)  9.13 us
    reshape x2, local copies, waits for them, and re-layouts, per_device(): outgoing = outgoing.reshape(dp_count, col_count, capacity, width)  9.13 us
    reshape x1, local copies, waits for them, and re-layouts, per_device(): token_rows = arrived.reshape(-1, width)  7.51 us
  transfers between devices with their start and end apart: 5, of which 2 were waited for; matrix products, arithmetic and copies ran while one was open for 6% of the time, Pallas kernels for 0%

commit v1 on v0

--- a/solution.py
+++ b/solution.py
@@ -47,8 +47,14 @@
     up_part = jnp.dot(token_rows, up_full, preferred_element_type=jnp.float32)
     hidden = (jax.nn.silu(gate_part) * up_part).astype(jnp.bfloat16)
     expert_out = jnp.dot(hidden, down_full, preferred_element_type=jnp.float32).astype(jnp.bfloat16)
-    returned = lax.all_to_all(
-        expert_out.reshape(shape_in), "expert", split_axis=1, concat_axis=1, tiled=True
+    returned = jnp.concatenate(
+        lax.all_to_all(
+            jnp.stack(jnp.split(expert_out.reshape(shape_in), lax.axis_size("expert"), axis=1)),
+            "expert",
+            0,
+            0,
+        ),
+        axis=1,
     )
     home = lax.all_to_all(returned, "dp", split_axis=0, concat_axis=0, tiled=True)
     home_flat = home.reshape(dev_count * capacity, width)

time: 336 us -> 351 us (1.045)
  local copies, waits for them, and re-layouts: 58.7 us -> 73.7 us
    unnamed x12 -> x27, local copies, waits for them, and re-layouts: 0.85 us -> 16.9 us
    reshape x2 -> x1, local copies, waits for them, and re-layouts: 9.13 us -> 4.43 us  [per_device(): expert_out.reshape(shape_in)]
    another operation x3 -> x5, local copies, waits for them, and re-layouts: 0.03 us -> 3.62 us  [the longest x2 3.59 us: per_device(): jnp.stack(jnp.split(expert_out.reshape(shape_in), lax.axis_size('expert')...]
where the time goes in v1:
time: 351 us; the launch traced here: 350 us
  blocking collectives  125 us (36%)
  waiting for transfers between devices  118 us (34%)
  local copies, waits for them, and re-layouts  73.7 us (21%)
  starting transfers between devices  15 us (4%)
  matrix products  12.8 us (4%)
  other arithmetic  5.1 us (1%)
    all_to_all x1, blocking collectives, per_device(): lax.all_to_all(jnp.stack(jnp.split(expert_out.reshape(shape_in), lax.axis...  78.7 us
    all_to_all x1, waiting for transfers between devices, per_device(): lax.all_to_all(first_section, 'expert', split_axis=1, concat_axis=1, tile...  70.3 us
    all_to_all x1, waiting for transfers between devices, per_device(): lax.all_to_all(returned, 'dp', split_axis=0, concat_axis=0, tiled=True)  48.1 us
    all_to_all x1, blocking collectives, per_device(): lax.all_to_all(outgoing, 'dp', split_axis=0, concat_axis=0, tiled=True)  46 us
    unnamed x27, local copies, waits for them, and re-layouts  16.9 us
    all_to_all x1, starting transfers between devices, per_device(): lax.all_to_all(first_section, 'expert', split_axis=1, concat_axis=1, tile...  10.5 us
    reshape x2, local copies, waits for them, and re-layouts, per_device(): outgoing = outgoing.reshape(dp_count, col_count, capacity, width)  9.13 us
    reshape x1, local copies, waits for them, and re-layouts, per_device(): token_rows = arrived.reshape(-1, width)  7.51 us
  transfers between devices with their start and end apart: 5, of which 2 were waited for; matrix products, arithmetic and copies ran while one was open for 6% of the time, Pallas kernels for 0%

profile of v1, /device:TPU:1, one launch (start us, length us, event | category | flops | bytes accessed | tf_op | source)
XLA Modules:
  0.0 350.1 jit_solution(1185155154330522591)
XLA Ops:
  2.2 4.6 %scatter_custom_fusion = bf16[768,2048]{1,0:T(8,128)(2,1)S(1)} fusion(s32[512]{0:T(512)S(1)} %bitcast.125, bf16[]{:T(256)} %constant.54.clone.1, bf16[64,2048]{1,0:T(8,128)(2,1)S(1)} %copy-done), kind=kCustom, calls=%fused_computation.17 | custom fusion | bytes 3407874 | tf_op jit(solution)/shard_map/scatter | solution.py:40
  6.8 4.4 %reshape.265 = bf16[16,16,3,2048]{3,2,1,0:T(4,128)(2,1)} reshape(bf16[768,2048]{1,0:T(8,128)(2,1)S(1)} %scatter_custom_fusion) | data formatting | bytes 6291456 | tf_op jit(solution)/shard_map/reshape | solution.py:41
  11.2 4.7 %copy.51 = bf16[16,16,3,2048]{3,1,2,0:T(8,128)(2,1)S(1)} copy(bf16[16,16,3,2048]{3,2,1,0:T(4,128)(2,1)} %reshape.265) | data formatting | bytes 6291456 | tf_op jit(solution)/shard_map/reshape | solution.py:41
  15.9 46.0 %all_to_all.20 = bf16[16,16,3,2048]{3,1,2,0:T(8,128)(2,1)S(1)} all-to-all(bf16[16,16,3,2048]{3,1,2,0:T(8,128)(2,1)S(1)} %copy.51), channel_id=1, replica_groups=mesh['dp'=16,'expert'=16] {'dp'}, dimensions={0} | all-to-all | bytes 6291456 | tf_op jit(solution)/shard_map/all_to_all | solution.py:42
  61.9 3.4 copy.52
  65.3 10.5 %all-to-all-start.1 = ((bf16[16,16,3,2048]{3,0,2,1:T(8,128)(2,1)}), bf16[16,16,3,2048]{3,0,2,1:T(8,128)(2,1)S(1)}, u32[]{:S(2)}, u32[]{:S(2)}) async-start(bf16[16,16,3,2048]{3,0,2,1:T(8,128)(2,1)} %copy.52), calls=%async_computation.1 | async-start | bytes 6291456 | tf_op jit(solution)/shard_map/all_to_all | solution.py:43
  76.5 70.3 %all-to-all-done.1 = bf16[16,16,3,2048]{3,0,2,1:T(8,128)(2,1)S(1)} async-done(((bf16[16,16,3,2048]{3,0,2,1:T(8,128)(2,1)}), bf16[16,16,3,2048]{3,0,2,1:T(8,128)(2,1)S(1)}, u32[]{:S(2)}, u32[]{:S(2)}) %all-to-all-start.1) | async-done | bytes 3145760 | tf_op jit(solution)/shard_map/all_to_all | solution.py:43
  146.8 4.6 %copy.53 = bf16[16,16,3,2048]{3,2,1,0:T(4,128)(2,1)} copy(bf16[16,16,3,2048]{3,0,2,1:T(8,128)(2,1)S(1)} %all-to-all-done.1) | data formatting | bytes 6291456 | tf_op jit(solution)/shard_map/all_to_all | solution.py:43
  151.4 7.5 %reshape.266 = bf16[768,2048]{1,0:T(8,128)(2,1)S(1)} reshape(bf16[16,16,3,2048]{3,2,1,0:T(4,128)(2,1)} %copy.53) | data formatting | bytes 6291456 | tf_op jit(solution)/shard_map/reshape | solution.py:45
  158.9 4.6 %fusion.1 = f32[768,768]{1,0:T(8,128)S(1)} fusion(bf16[768,2048]{1,0:T(8,128)(2,1)S(1)} %reshape.266, bf16[2048,384]{1,0:T(8,128)(2,1)} %collective-permute-done, bf16[2048,384]{1,0:T(8,128)(2,1)} %bitcast.129), kind=kOutput, calls=%fused_computation.5 | convolution fusion | flops 2422210560 | bytes 8650752 | tf_op jit(solution)/shard_map/dot_general | solution.py:46
  163.5 4.1 %fusion.5 = f32[768,768]{1,0:T(8,128)S(1)} fusion(bf16[768,2048]{1,0:T(8,128)(2,1)S(1)} %reshape.266, bf16[2048,384]{1,0:T(8,128)(2,1)} %collective-permute-done.1, bf16[2048,384]{1,0:T(8,128)(2,1)S(1)} %bitcast.131), kind=kOutput, calls=%fused_computation.9 | convolution fusion | flops 2422210560 | bytes 8650752 | tf_op jit(solution)/shard_map/dot_general | solution.py:47
  167.7 4.1 %convolution_convert_fusion = bf16[768,2048]{1,0:T(8,128)(2,1)S(1)} fusion(bf16[384,2048]{1,0:T(8,128)(2,1)} %collective-permute-done.2, bf16[384,2048]{1,0:T(8,128)(2,1)S(1)} %bitcast.133, f32[768,768]{1,0:T(8,128)S(1)} %fusion.5, f32[768,768]{1,0:T(8,128)S(1)} %fusion.1), kind=kOutput, calls=%fused_computation.4 | convolution fusion | flops 2427322368 | bytes 11010048 | tf_op jit(solution)/shard_map/dot_general | solution.py:49
  171.8 4.4 %reshape.267 = bf16[16,16,3,2048]{3,2,1,0:T(4,128)(2,1)} reshape(bf16[768,2048]{1,0:T(8,128)(2,1)S(1)} %convolution_convert_fusion) | data formatting | bytes 6291456 | tf_op jit(solution)/shard_map/reshape | solution.py:52
  178.3 1.1 fusion.31
  179.4 1.1 fusion.30
  193.5 2.5 copy.69
  196.0 78.7 %all_to_all.21 = bf16[16,16,1,3,2048]{4,1,3,2,0:T(8,128)(2,1)S(1)} all-to-all(bf16[16,16,1,3,2048]{4,1,3,2,0:T(8,128)(2,1)S(1)} %copy.69), channel_id=1, replica_groups=mesh['dp'=16,'expert'=16] {'expert'}, dimensions={0} | all-to-all | bytes 6291456 | tf_op jit(solution)/shard_map/all_to_all | solution.py:51
  274.8 3.4 copy.70
  278.1 3.9 %all-to-all-start.3 = ((bf16[16,16,3,2048]{3,1,2,0:T(8,128)(2,1)}), bf16[16,16,3,2048]{3,1,2,0:T(8,128)(2,1)S(1)}, u32[]{:S(2)}, u32[]{:S(2)}) async-start(bf16[16,16,3,2048]{3,1,2,0:T(8,128)(2,1)} %copy.70), calls=%async_computation.3 | async-start | bytes 6291456 | tf_op jit(solution)/shard_map/all_to_all | solution.py:59
  282.2 48.1 %all-to-all-done.3 = bf16[16,16,3,2048]{3,1,2,0:T(8,128)(2,1)S(1)} async-done(((bf16[16,16,3,2048]{3,1,2,0:T(8,128)(2,1)}), bf16[16,16,3,2048]{3,1,2,0:T(8,128)(2,1)S(1)}, u32[]{:S(2)}, u32[]{:S(2)}) %all-to-all-start.3) | async-done | bytes 3145760 | tf_op jit(solution)/shard_map/all_to_all | solution.py:59
  330.3 4.7 %copy.71 = bf16[16,16,3,2048]{3,2,1,0:T(4,128)(2,1)} copy(bf16[16,16,3,2048]{3,1,2,0:T(8,128)(2,1)S(1)} %all-to-all-done.3) | data formatting | bytes 6291456 | tf_op jit(solution)/shard_map/all_to_all | solution.py:59
  335.0 7.5 %reshape.270 = bf16[768,2048]{1,0:T(8,128)(2,1)S(1)} reshape(bf16[16,16,3,2048]{3,2,1,0:T(4,128)(2,1)} %copy.71) | data formatting | bytes 6291456 | tf_op jit(solution)/shard_map/reshape | solution.py:60
  342.5 3.3 gather_fusion
  345.8 4.2 %fusion = f32[64,2048]{1,0:T(8,128)} fusion(bf16[512,2048]{1,0:T(8,128)(2,1)} %gather_fusion, f32[64,8]{1,0:T(8,128)S(1)} %copy.72), kind=kLoop, calls=%fused_computation.3 | loop fusion | flops 3014656 | bytes 2623488 | tf_op jit(solution)/shard_map/reduce_sum | solution.py:62
  (48 shorter events, 18.0 us)
Async XLA Ops:
  0.0 2.2 copy-start
  65.3 81.4 %all-to-all-start.1 = ((bf16[16,16,3,2048]{3,0,2,1:T(8,128)(2,1)}), bf16[16,16,3,2048]{3,0,2,1:T(8,128)(2,1)S(1)}, u32[]{:S(2)}, u32[]{:S(2)}) async-start(bf16[16,16,3,2048]{3,0,2,1:T(8,128)(2,1)} %copy.52), calls=%async_computation.1 | async-start | bytes 6291456 | tf_op jit(solution)/shard_map/all_to_all | solution.py:43
  75.8 83.1 %collective-permute-start = (bf16[2048,384]{1,0:T(8,128)(2,1)}, bf16[2048,384]{1,0:T(8,128)(2,1)}, u32[]{:S(2)}, u32[]{:S(2)}) collective-permute-start(bf16[2048,384]{1,0:T(8,128)(2,1)} %bitcast.128), channel_id=1, source_target_pairs={{0,1},{1,0},{2,3},{3,2},{4,5},{5,4},{6,7},{7,6},{8,9},{9,8},{10,11... | collective-permute-start | bytes 4718600 | tf_op jit(solution)/shard_map/ppermute | solution.py:8
  76.0 87.6 %collective-permute-start.1 = (bf16[2048,384]{1,0:T(8,128)(2,1)}, bf16[2048,384]{1,0:T(8,128)(2,1)}, u32[]{:S(2)}, u32[]{:S(2)}) collective-permute-start(bf16[2048,384]{1,0:T(8,128)(2,1)} %bitcast.130), channel_id=1, source_target_pairs={{0,1},{1,0},{2,3},{3,2},{4,5},{5,4},{6,7},{7,6},{8,9},{9,8},{10,11... | collective-permute-start | bytes 4718600 | tf_op jit(solution)/shard_map/ppermute | solution.py:8
  76.3 91.4 %collective-permute-start.2 = (bf16[384,2048]{1,0:T(8,128)(2,1)}, bf16[384,2048]{1,0:T(8,128)(2,1)}, u32[]{:S(2)}, u32[]{:S(2)}) collective-permute-start(bf16[384,2048]{1,0:T(8,128)(2,1)} %bitcast.132), channel_id=1, source_target_pairs={{0,1},{1,0},{2,3},{3,2},{4,5},{5,4},{6,7},{7,6},{8,9},{9,8},{10,11... | collective-permute-start | bytes 4718600 | tf_op jit(solution)/shard_map/ppermute | solution.py:8
  158.9 4.6 %copy-start.3 = (bf16[1,2048,384]{2,1,0:T(8,128)(2,1)S(1)}, bf16[1,2048,384]{2,1,0:T(8,128)(2,1)}, u32[]{:S(2)}) copy-start(bf16[1,2048,384]{2,1,0:T(8,128)(2,1)} %param.10) | copy-start | bytes 4718596
  163.5 4.2 %copy-start.4 = (bf16[1,384,2048]{2,1,0:T(8,128)(2,1)S(1)}, bf16[1,384,2048]{2,1,0:T(8,128)(2,1)}, u32[]{:S(2)}) copy-start(bf16[1,384,2048]{2,1,0:T(8,128)(2,1)} %param.11) | copy-start | bytes 4718596
  278.1 3.9 %copy-start.2 = (s32[64,8]{0,1:T(8,128)S(1)}, s32[64,8]{0,1:T(8,128)}, u32[]{:S(2)}) copy-start(s32[64,8]{0,1:T(8,128)} %param.8) | copy-start | bytes 6148
  278.1 52.1 %all-to-all-start.3 = ((bf16[16,16,3,2048]{3,1,2,0:T(8,128)(2,1)}), bf16[16,16,3,2048]{3,1,2,0:T(8,128)(2,1)S(1)}, u32[]{:S(2)}, u32[]{:S(2)}) async-start(bf16[16,16,3,2048]{3,1,2,0:T(8,128)(2,1)} %copy.70), calls=%async_computation.3 | async-start | bytes 6291456 | tf_op jit(solution)/shard_map/all_to_all | solution.py:59
  342.5 7.6 %copy-start.1 = (bf16[64,2048]{1,0:T(8,128)(2,1)S(1)}, bf16[64,2048]{1,0:T(8,128)(2,1)}, u32[]{:S(2)}) copy-start(bf16[64,2048]{1,0:T(8,128)(2,1)} %param.6) | copy-start | bytes 786436
